TPU v7x, 256 devices: a whole 4x4x8 slice. The times are simulated.
256 devices in a mesh: freq: 8 (over z), lat: 8 (over x, y_hi), lon: 4 (over y_lo, core).
Axes of the slice: x: 4, y: 4 (y_hi: 2, y_lo: 2; y = y_hi * 2 + y_lo), z: 8, core: 2. Of those that a mesh axis runs over, the one named last changes fastest.
Arguments:
- direction: float32 [3, 32, 1024, 2048], P(None, 'freq', 'lat', 'lon'), may hold values from -6 to 6
- base_flow: float32 [2, 32, 1024, 2048], P(None, 'freq', 'lat', 'lon'), may hold values from -2 to 2
- water_depth: float32 [1024, 2048], P('lat', 'lon'), may hold values from 0.5 to 2
- drag_factor: float32 [1024, 2048], P('lat', 'lon'), may hold values from 0.2 to 2
- wet_mask: int32 [1024, 2048], P('lat', 'lon'), may hold values 0 or 1
Outputs:
- result: float32 [3, 32, 1024, 2048], P(None, 'freq', 'lat', 'lon')
All inputs are finite; a program needn't handle non-finite values. No bound on the sum of `wet_mask` on one device may be relied on, other than what follows from the above.
Results may differ from a plain program's by a relative error of at most 0.000071.
Values sent between devices are 32-bit elements; how exact they have to be, the bound alone decides.
A program may use at most 128 MiB of HBM per device.

v0:
```python
import math
import jax
import jax.numpy as jnp
from jax import lax
from jax.sharding import PartitionSpec as P

NCON = 16
NTIME = 256
LINEAR_DRAG = 0.5
GRAVITY = 1.0
OMEGA_STEP = 0.25
SPEED_SOFT = 0.01


def extended_2(block, sides, width):
    for axis, dim in sides:
        count = lax.axis_size(axis)
        forward = [(i, i + 1) for i in range(count - 1)]
        forward.append((count - 1, 0))
        backward = [(target, source) for source, target in forward]
        low = lax.ppermute(
            lax.slice_in_dim(block, block.shape[dim] - width, None, axis=dim), axis, forward
        )
        high = lax.ppermute(lax.slice_in_dim(block, 0, width, axis=dim), axis, backward)
        block = jnp.concatenate([low, block, high], axis=dim)
    return block


def samples_table(sample_count, constituents):
    sample_index = jnp.arange(sample_count, dtype=jnp.int32)
    harmonic = jnp.arange(1, constituents + 1, dtype=jnp.int32)
    wrapped_turns = sample_index[:, None] * harmonic[None, :] % sample_count
    phase_angle = wrapped_turns.astype(jnp.float32) * (2.0 * math.pi / sample_count)
    table = jnp.stack([jnp.cos(phase_angle), jnp.sin(phase_angle)], axis=2)
    return table.reshape(sample_count, 2 * constituents)


def rotation_of(row_index, total_rows):
    return 0.5 + (row_index.astype(jnp.float32) + 0.5) / total_rows


def tendency(values, angular):
    cos_sin = values.reshape((values.shape[0] // 2, 2) + values.shape[1:])
    moved = jnp.stack([angular * cos_sin[:, 1], -angular * cos_sin[:, 0]], axis=1)
    return moved.reshape(values.shape)


def linear_residual(extended, tile_rows, tile_cols, angular, rotation):

    def neighbour(plane, row_step, col_step):
        return extended[
            plane,
            :,
            1 + row_step : 1 + row_step + tile_rows,
            1 + col_step : 1 + col_step + tile_cols,
        ]

    height = neighbour(0, 0, 0)
    east = neighbour(1, 0, 0)
    north = neighbour(2, 0, 0)
    res_height = (
        tendency(height, angular)
        + neighbour(3, 0, 0)
        - neighbour(3, 0, -1)
        + neighbour(4, 0, 0)
        - neighbour(4, -1, 0)
    )
    north_mean = 0.25 * (north + neighbour(2, 0, 1) + neighbour(2, -1, 0) + neighbour(2, -1, 1))
    east_mean = 0.25 * (east + neighbour(1, 0, -1) + neighbour(1, 1, 0) + neighbour(1, 1, -1))
    res_east = (
        tendency(east, angular)
        + LINEAR_DRAG * east
        - rotation * north_mean
        + GRAVITY * (neighbour(0, 0, 1) - height)
    )
    res_north = (
        tendency(north, angular)
        + LINEAR_DRAG * north
        + rotation * east_mean
        + GRAVITY * (neighbour(0, 1, 0) - height)
    )
    return jnp.stack([res_height, res_east, res_north])


def friction_row(row_block, drag_row, table):
    highest = lax.Precision.HIGHEST
    series = jnp.einsum("tc,fcn->ftn", table, row_block, precision=highest)
    base_east, base_north, step_east, step_north = (series[0], series[1], series[2], series[3])
    magnitude = jnp.sqrt(base_east * base_east + base_north * base_north + SPEED_SOFT)
    projected = (base_east * step_east + base_north * step_north) / magnitude
    force_east = drag_row * (magnitude * step_east + base_east * projected)
    force_north = drag_row * (magnitude * step_north + base_north * projected)
    forces = jnp.stack([force_east, force_north])
    analysed = jnp.einsum("tc,ftn->fcn", table, forces, precision=highest) * (2.0 / table.shape[0])
    drag_rate = drag_row * jnp.mean(magnitude, axis=0)
    return (analysed, drag_rate)


def precondition(residual, angular, rotation, drag_rate):
    shaped = residual.reshape((3, residual.shape[1] // 2, 2) + residual.shape[2:])
    cos_part = shaped[:, :, 0]
    sin_part = shaped[:, :, 1]
    height_cos = -sin_part[0] / angular
    height_sin = cos_part[0] / angular
    real_rate = drag_rate + LINEAR_DRAG
    det_real = real_rate * real_rate - angular * angular + rotation * rotation
    det_imag = 2.0 * real_rate * angular
    det_norm = det_real * det_real + det_imag * det_imag
    inv_real = det_real / det_norm
    inv_imag = -det_imag / det_norm
    east_re = cos_part[1]
    east_im = -sin_part[1]
    north_re = cos_part[2]
    north_im = -sin_part[2]
    num_east_re = real_rate * east_re - angular * east_im + rotation * north_re
    num_east_im = real_rate * east_im + angular * east_re + rotation * north_im
    num_north_re = -rotation * east_re + real_rate * north_re - angular * north_im
    num_north_im = -rotation * east_im + real_rate * north_im + angular * north_re
    east_out_re = num_east_re * inv_real - num_east_im * inv_imag
    east_out_im = num_east_re * inv_imag + num_east_im * inv_real
    north_out_re = num_north_re * inv_real - num_north_im * inv_imag
    north_out_im = num_north_re * inv_imag + num_north_im * inv_real
    cosines = jnp.stack([height_cos, east_out_re, north_out_re])
    sines = jnp.stack([height_sin, -east_out_im, -north_out_im])
    return jnp.stack([cosines, sines], axis=2).reshape(residual.shape)


def local(direction, base_flow, water_depth, drag_factor, wet_mask):
    local_coefs = direction.shape[1]
    tile_rows = direction.shape[2]
    tile_cols = direction.shape[3]
    groups = lax.axis_size("freq")
    member = lax.axis_index("freq")
    band_rows = tile_rows // groups
    lat_place = lax.axis_index("lat")
    lat_count = lax.axis_size("lat")
    total_rows = tile_rows * lat_count
    wet_cells = wet_mask.astype(jnp.float32)
    height = direction[0] * wet_cells
    east = direction[1] * wet_cells
    north = direction[2] * wet_cells
    planes = jnp.stack([height, east, north, water_depth * east, water_depth * north])
    extended = extended_2(planes, (("lat", 2), ("lon", 3)), 1)
    rim_keep = jnp.ones((tile_rows + 2,), jnp.float32)
    rim_keep = rim_keep.at[0].set(jnp.where(lat_place == 0, 0.0, 1.0))
    rim_keep = rim_keep.at[tile_rows + 1].set(jnp.where(lat_place == lat_count - 1, 0.0, 1.0))
    extended = extended * rim_keep[:, None]
    local_count = local_coefs // 2
    first_con = member * local_count
    angular_local = OMEGA_STEP * (first_con + jnp.arange(local_count, dtype=jnp.int32) + 1).astype(
        jnp.float32
    )
    row_global = lat_place * tile_rows + jnp.arange(tile_rows, dtype=jnp.int32)
    rotation = rotation_of(row_global, total_rows)
    linear_part = linear_residual(
        extended, tile_rows, tile_cols, angular_local[:, None, None], rotation[:, None]
    )
    table = samples_table(NTIME, NCON)
    flows = jnp.concatenate([base_flow, jnp.stack([east, north])], axis=0)
    band_start = member * band_rows
    drag_band = lax.dynamic_slice_in_dim(drag_factor, band_start, band_rows, 0)
    flows_band, linear_band = (
        lax.all_to_all(flows, "freq", split_axis=2, concat_axis=1, tiled=True),
        lax.all_to_all(linear_part, "freq", split_axis=2, concat_axis=1, tiled=True),
    )
    mask_band = lax.dynamic_slice_in_dim(wet_cells, band_start, band_rows, 0)
    rotation_band = rotation_of(
        lat_place * tile_rows + band_start + jnp.arange(band_rows, dtype=jnp.int32), total_rows
    )
    angular_all = OMEGA_STEP * jnp.arange(1, NCON + 1, dtype=jnp.float32)

    def finish_row(items):
        row_block, linear_row, drag_row, mask_row, rotation_row = items
        friction, drag_rate = friction_row(row_block, drag_row, table)
        residual = (
            linear_row + jnp.concatenate([jnp.zeros_like(friction[:1]), friction], axis=0)
        ) * mask_row
        return precondition(residual, angular_all[:, None], rotation_row, drag_rate)

    band_result = lax.map(
        finish_row,
        (
            jnp.moveaxis(flows_band, 2, 0),
            jnp.moveaxis(linear_band, 2, 0),
            drag_band,
            mask_band,
            rotation_band,
        ),
    )
    band_result = jnp.moveaxis(band_result, 0, 2)
    return lax.all_to_all(band_result, "freq", split_axis=1, concat_axis=2, tiled=True)


def solution(mesh):
    placed = (
        P(None, "freq", "lat", "lon"),
        P(None, "freq", "lat", "lon"),
        P("lat", "lon"),
        P("lat", "lon"),
        P("lat", "lon"),
    )
    return jax.shard_map(
        local, mesh=mesh, in_specs=placed, out_specs=P(None, "freq", "lat", "lon"), check_vma=False
    )
```

profile of v0, /device:TPU:2, one launch (start us, length us, event | category | flops | bytes accessed | tf_op | source)
XLA Modules:
  0.0 540.5 jit_solution(4843827294149295579)
XLA Ops:
  6.0 2.4 copy-done
  8.5 3.3 collective-permute-start
  26.5 5.9 %maximum_multiply_fusion = f32[5,4,130,514]{3,2,1,0:T(8,128)S(1)} fusion(f32[5,4,130,1]{3,2,1,0:T(8,128)S(1)} %copy.113, f32[5,4,1,512]{3,2,1,0:T(1,128)S(1)} %copy.109, f32[5,4,128,512]{3,2,1,0:T(8,128)} %copy-done, f32[5,4,1,512]{3,2,1,0:T(1,128)S(1)} %copy.108, f32[5,4,130,1]{3,2,1,0:T(8,128)S(1)} %copy.112, f32[130]{0:T(256)S(1)} %constant_dynamic-update-slice_fusion.2), kind=kLoop, calls=%fused_computation.57 | loop fusion | flops 6682000 | bytes 10691720 | tf_op jit(solution)/shard_map/mul | solution.py:147
  35.4 2.7 fusion.27
  38.4 3.7 copy.114
  42.1 8.5 %all-to-all-start = ((f32[3,4,128,512]{3,1,0,2:T(4,128)}), f32[3,4,128,512]{3,1,0,2:T(4,128)S(1)}, u32[]{:S(2)}, u32[]{:S(2)}) async-start(f32[3,4,128,512]{3,1,0,2:T(4,128)} %copy.114), calls=%async_computation | async-start | bytes 6291456 | tf_op jit(solution)/shard_map/all_to_all | solution.py:164
  55.9 2.7 pad_maximum_fusion.1
  58.5 66.9 %all-to-all-done = f32[3,4,128,512]{3,1,0,2:T(4,128)S(1)} async-done(((f32[3,4,128,512]{3,1,0,2:T(4,128)}), f32[3,4,128,512]{3,1,0,2:T(4,128)S(1)}, u32[]{:S(2)}, u32[]{:S(2)}) %all-to-all-start) | async-done | bytes 3145760 | tf_op jit(solution)/shard_map/all_to_all | solution.py:164
  125.5 4.6 all-to-all-start.1
  131.1 2.7 copy.115
  133.8 4.9 all_to_all.42
  138.7 88.1 %all-to-all-done.1 = f32[4,4,128,512]{3,1,0,2:T(4,128)} async-done(((f32[4,4,128,512]{3,1,0,2:T(4,128)}), f32[4,4,128,512]{3,1,0,2:T(4,128)}, u32[]{:S(2)}, u32[]{:S(2)}) %all-to-all-start.1) | async-done | bytes 4194336 | tf_op jit(solution)/shard_map/all_to_all | solution.py:163
  226.8 5.4 %copy.119 = f32[4,8,4,16,512]{4,2,1,0,3:T(4,128)} copy(f32[4,8,4,16,512]{4,2,0,3,1:T(4,128)} %bitcast.12) | data formatting | bytes 8388608 | tf_op jit(solution)/shard_map/all_to_all | solution.py:163
  232.2 5.3 all_to_all.46
  237.5 225.6 %while.15 = (s32[]{:T(128)}, f32[16,3,32,512]{3,0,1,2:T(8,128)}, f32[16,3,32,512]{3,2,1,0:T(8,128)}, f32[16,512]{1,0:T(8,128)S(1)}, f32[16,4,32,512]{3,2,1,0:T(8...) while((s32[]{:T(128)}, f32[16,3,32,512]{3,0,1,2:T(8,128)}, ...), condition=%wide.region_2.3_spmd.clone.clone, body=%wide.region_0.0_spmd.clone.clone.sunk | while | flops 305752128 | bytes 11770913 | solution.py:180
  237.5 2.9 convolution_bitcast_fusion.2
  246.6 5.0 dynamic_update_slice.8
  251.6 2.9 convolution_bitcast_fusion.2
  260.7 5.0 dynamic_update_slice.8
  265.7 2.9 convolution_bitcast_fusion.2
  274.8 5.0 dynamic_update_slice.8
  279.8 2.9 convolution_bitcast_fusion.2
  288.9 5.0 dynamic_update_slice.8
  293.8 2.9 convolution_bitcast_fusion.2
  303.0 5.0 dynamic_update_slice.8
  307.9 2.9 convolution_bitcast_fusion.2
  317.1 5.0 dynamic_update_slice.8
  322.0 2.9 convolution_bitcast_fusion.2
  331.2 5.0 dynamic_update_slice.8
  336.1 2.9 convolution_bitcast_fusion.2
  345.3 5.0 dynamic_update_slice.8
  350.2 2.9 convolution_bitcast_fusion.2
  359.4 5.0 dynamic_update_slice.8
  364.3 2.9 convolution_bitcast_fusion.2
  373.5 5.0 dynamic_update_slice.8
  378.4 2.9 convolution_bitcast_fusion.2
  387.5 5.0 dynamic_update_slice.8
  392.5 2.9 convolution_bitcast_fusion.2
  401.6 5.0 dynamic_update_slice.8
  406.6 2.9 convolution_bitcast_fusion.2
  415.7 5.0 dynamic_update_slice.8
  420.7 2.9 convolution_bitcast_fusion.2
  429.8 5.0 dynamic_update_slice.8
  434.8 2.9 convolution_bitcast_fusion.2
  443.9 5.0 dynamic_update_slice.8
  448.9 2.9 convolution_bitcast_fusion.2
  458.0 5.0 dynamic_update_slice.8
  463.0 75.5 %all_to_all.54 = f32[3,32,16,512]{3,2,0,1:T(8,128)S(1)} all-to-all(f32[3,32,16,512]{3,2,0,1:T(8,128)} %bitcast.160), channel_id=1, replica_groups=mesh['freq'=8,'lat'=8,'lon'=4] {'freq'}, dimensions={1} | all-to-all | bytes 6291456 | tf_op jit(solution)/shard_map/all_to_all | solution.py:191
  (360 shorter events, 102.9 us)
Async XLA Ops:
  2.3 3.4 copy-start.4
  3.9 2.2 copy-start.1
  5.7 2.7 copy-start.2
  6.0 2.4 copy-start
  8.5 6.7 %collective-permute-start = (f32[5,4,1,512]{3,0,2,1:T(8,128)S(1)}, f32[5,4,1,512]{3,0,2,1:T(8,128)S(1)}, u32[]{:S(2)}, u32[]{:S(2)}) collective-permute-start(f32[5,4,1,512]{3,0,2,1:T(8,128)S(1)} %copy.106), channel_id=1, source_target_pairs={{0,4},{4,8},{8,12},{12,16},{16,20},{20,24},{24,28},{28,0},{1,5},{5... | collective-permute-start | bytes 122888 | tf_op jit(solution)/shard_map/ppermute | solution.py:21
  11.8 5.8 %collective-permute-start.1 = (f32[5,4,1,512]{3,0,2,1:T(8,128)S(1)}, f32[5,4,1,512]{3,0,2,1:T(8,128)S(1)}, u32[]{:S(2)}, u32[]{:S(2)}) collective-permute-start(f32[5,4,1,512]{3,0,2,1:T(8,128)S(1)} %copy.107), channel_id=1, source_target_pairs={{4,0},{8,4},{12,8},{16,12},{20,16},{24,20},{28,24},{0,28},{5,1},{9... | collective-permute-start | bytes 122888 | tf_op jit(solution)/shard_map/ppermute | solution.py:24
  21.2 3.4 collective-permute-start.2
  22.4 3.6 collective-permute-start.3
  42.1 83.4 %all-to-all-start = ((f32[3,4,128,512]{3,1,0,2:T(4,128)}), f32[3,4,128,512]{3,1,0,2:T(4,128)S(1)}, u32[]{:S(2)}, u32[]{:S(2)}) async-start(f32[3,4,128,512]{3,1,0,2:T(4,128)} %copy.114), calls=%async_computation | async-start | bytes 6291456 | tf_op jit(solution)/shard_map/all_to_all | solution.py:164
  50.6 4.0 copy-start.3
  125.5 101.3 %all-to-all-start.1 = ((f32[4,4,128,512]{3,1,0,2:T(4,128)}), f32[4,4,128,512]{3,1,0,2:T(4,128)}, u32[]{:S(2)}, u32[]{:S(2)}) async-start(f32[4,4,128,512]{3,1,0,2:T(4,128)} %pad_maximum_fusion.1), calls=%async_computation.1 | async-start | bytes 8388608 | tf_op jit(solution)/shard_map/all_to_all | solution.py:163
where the time goes:
time: 544 us; the launch traced here: 541 us
  waiting for transfers between devices  161 us (30%)
  local copies, waits for them, and re-layouts  136 us (25%)
  blocking collectives  75.5 us (14%)
  other arithmetic  61.9 us (11%)
  matrix products  57.8 us (11%)
  loops' own time  29.1 us (5%)
  starting transfers between devices  19.6 us (4%)
    all_to_all x1, waiting for transfers between devices, local(): lax.all_to_all(flows, 'freq', split_axis=2, concat_axis=1, tiled=True)  88.1 us
    dynamic_update_slice x48, local copies, waits for them, and re-layouts, local(): lax.map(finish_row, (jnp.moveaxis(flows_band, 2, 0), jnp.moveaxis(linear_...  86.2 us
    all_to_all x1, blocking collectives, local(): lax.all_to_all(band_result, 'freq', split_axis=1, concat_axis=2, tiled=True)  75.5 us
    all_to_all x1, waiting for transfers between devices, local(): lax.all_to_all(linear_part, 'freq', split_axis=2, concat_axis=1, tiled=True)  66.9 us
    dot_general x16, matrix products, friction_row(): series = jnp.einsum('tc,fcn->ftn', table, row_block, precision=highest)  46.2 us
    another operation x1, loops' own time, local(): lax.map(finish_row, (jnp.moveaxis(flows_band, 2, 0), jnp.moveaxis(linear_...  29.1 us
    mul x16, other arithmetic, finish_row(): (linear_row + jnp.concatenate([jnp.zeros_like(friction[:1]), friction], a...  15.4 us
    dot_general x16, matrix products, friction_row(): jnp.einsum('tc,ftn->fcn', table, forces, precision=highest)  11.7 us
  transfers between devices with their start and end apart: 6, of which 6 were waited for; matrix products, arithmetic and copies ran while one was open for 2% of the time, Pallas kernels for 0%

commit v1 on v0

--- a/solution.py
+++ b/solution.py
@@ -188,7 +188,12 @@
         ),
     )
     band_result = jnp.moveaxis(band_result, 0, 2)
-    return lax.all_to_all(band_result, "freq", split_axis=1, concat_axis=2, tiled=True)
+    return jnp.concatenate(
+        lax.all_to_all(
+            jnp.stack(jnp.split(band_result, lax.axis_size("freq"), axis=1)), "freq", 0, 0
+        ),
+        axis=2,
+    )
 
 
 def solution(mesh):

time: 544 us -> 494 us (0.908)
  local copies, waits for them, and re-layouts: 136 us -> 71.6 us
  matrix products: 57.8 us -> 70 us
    dynamic_update_slice x48 -> x16, local copies, waits for them, and re-layouts: 86.2 us -> 11.1 us  [local(): lax.map(finish_row, (jnp.moveaxis(flows_band, 2, 0), jnp.moveaxis(linear_...]
    mul x16, other arithmetic: 15.4 us -> 0.49 us  [finish_row(): (linear_row + jnp.concatenate([jnp.zeros_like(friction[:1]), friction], a...]
    dot_general x16, matrix products: 11.7 us -> 23.8 us  [friction_row(): jnp.einsum('tc,ftn->fcn', table, forces, precision=highest)]
    mul x16, other arithmetic: 0.29 us -> 12 us  [precondition(): det_real = real_rate * real_rate - angular * angular + rotation * rotation]
  transfers between devices with their start and end apart: 6 -> 6, of which waited for: 6 -> 6; matrix products, arithmetic and copies ran while one was open for 2% -> 3% of each run, Pallas kernels for 0% -> 0%
where the time goes in v1:
time: 494 us; the launch traced here: 490 us
  waiting for transfers between devices  161 us (33%)
  blocking collectives  75.3 us (15%)
  local copies, waits for them, and re-layouts  71.6 us (14%)
  matrix products  70 us (14%)
  other arithmetic  59.8 us (12%)
  loops' own time  32.2 us (7%)
  starting transfers between devices  19.6 us (4%)
    all_to_all x1, waiting for transfers between devices, local(): lax.all_to_all(flows, 'freq', split_axis=2, concat_axis=1, tiled=True)  88.6 us
    all_to_all x1, blocking collectives, local(): lax.all_to_all(jnp.stack(jnp.split(band_result, lax.axis_size('freq'), ax...  75.3 us
    all_to_all x1, waiting for transfers between devices, local(): lax.all_to_all(linear_part, 'freq', split_axis=2, concat_axis=1, tiled=True)  66.9 us
    dot_general x16, matrix products, friction_row(): series = jnp.einsum('tc,fcn->ftn', table, row_block, precision=highest)  46.2 us
    another operation x1, loops' own time, local(): lax.map(finish_row, (jnp.moveaxis(flows_band, 2, 0), jnp.moveaxis(linear_...  32.2 us
    dot_general x16, matrix products, friction_row(): jnp.einsum('tc,ftn->fcn', table, forces, precision=highest)  23.8 us
    mul x16, other arithmetic, precondition(): det_real = real_rate * real_rate - angular * angular + rotation * rotation  12 us
    sub x16, other arithmetic, precondition(): east_out_re = num_east_re * inv_real - num_east_im * inv_imag  11.7 us
  transfers between devices with their start and end apart: 6, of which 6 were waited for; matrix products, arithmetic and copies ran while one was open for 3% of the time, Pallas kernels for 0%

profile of v1, /device:TPU:2, one launch (start us, length us, event | category | flops | bytes accessed | tf_op | source)
XLA Modules:
  0.0 489.9 jit_solution(18152999448794091365)
XLA Ops:
  2.3 1.5 constant_dynamic-update-slice_fusion.2
  3.9 1.9 constant_dynamic-update-slice_fusion.1
  6.0 2.3 copy-done
  8.5 3.3 collective-permute-start
  13.1 2.1 collective-permute-done
  15.3 2.3 collective-permute-done.1
  17.7 2.3 pad_maximum_fusion.5
  22.4 2.0 collective-permute-start.3
  26.5 5.9 %maximum_multiply_fusion = f32[5,4,130,514]{3,2,1,0:T(8,128)S(1)} fusion(f32[5,4,130,1]{3,2,1,0:T(8,128)S(1)} %copy.109, f32[5,4,1,512]{3,2,1,0:T(1,128)S(1)} %copy.105, f32[5,4,128,512]{3,2,1,0:T(8,128)} %copy-done, f32[5,4,1,512]{3,2,1,0:T(1,128)S(1)} %copy.104, f32[5,4,130,1]{3,2,1,0:T(8,128)S(1)} %copy.108, f32[130]{0:T(256)S(1)} %constant_dynamic-update-slice_fusion.3), kind=kLoop, calls=%fused_computation.58 | loop fusion | flops 6682000 | bytes 10691720 | tf_op jit(solution)/shard_map/mul | solution.py:147
  33.1 1.8 slice_subtract_fusion.2
  35.4 2.7 fusion.27
  38.4 3.7 copy.110
  42.1 8.5 %all-to-all-start = ((f32[3,4,128,512]{3,1,0,2:T(4,128)}), f32[3,4,128,512]{3,1,0,2:T(4,128)S(1)}, u32[]{:S(2)}, u32[]{:S(2)}) async-start(f32[3,4,128,512]{3,1,0,2:T(4,128)} %copy.110), calls=%async_computation | async-start | bytes 6291456 | tf_op jit(solution)/shard_map/all_to_all | solution.py:164
  50.6 2.1 copy.114
  52.6 1.9 copy.113
  55.9 2.7 pad_maximum_fusion.1
  58.6 66.9 %all-to-all-done = f32[3,4,128,512]{3,1,0,2:T(4,128)S(1)} async-done(((f32[3,4,128,512]{3,1,0,2:T(4,128)}), f32[3,4,128,512]{3,1,0,2:T(4,128)S(1)}, u32[]{:S(2)}, u32[]{:S(2)}) %all-to-all-start) | async-done | bytes 3145760 | tf_op jit(solution)/shard_map/all_to_all | solution.py:164
  125.5 4.6 all-to-all-start.1
  132.3 2.7 copy.111
  134.9 3.2 all_to_all.32
  138.1 88.6 %all-to-all-done.1 = f32[4,4,128,512]{3,1,0,2:T(4,128)} async-done(((f32[4,4,128,512]{3,1,0,2:T(4,128)}), f32[4,4,128,512]{3,1,0,2:T(4,128)}, u32[]{:S(2)}, u32[]{:S(2)}) %all-to-all-start.1) | async-done | bytes 4194336 | tf_op jit(solution)/shard_map/all_to_all | solution.py:163
  226.8 5.4 %copy.115 = f32[4,8,4,16,512]{4,2,1,0,3:T(4,128)} copy(f32[4,8,4,16,512]{4,2,0,3,1:T(4,128)} %bitcast.12) | data formatting | bytes 8388608 | tf_op jit(solution)/shard_map/all_to_all | solution.py:163
  232.2 5.3 %all_to_all.36 = f32[4,32,16,512]{3,1,0,2:T(8,128)} reshape(f32[4,8,4,16,512]{4,2,1,0,3:T(4,128)} %copy.115) | data formatting | bytes 8388608 | tf_op jit(solution)/shard_map/all_to_all | solution.py:163
  237.5 169.0 %while.15 = (s32[]{:T(128)}, f32[16,3,32,512]{3,2,1,0:T(8,128)}, f32[16,3,32,512]{3,2,1,0:T(8,128)S(1)}, f32[16,512]{1,0:T(8,128)}, f32[16,4,32,512]{3,2,1,0:T(8...) while((s32[]{:T(128)}, f32[16,3,32,512]{3,2,1,0:T(8,128)}, ...), condition=%wide.region_2.3_spmd.clone.clone, body=%wide.region_0.0_spmd.clone.clone.sunk | while | flops 305752128 | bytes 11771413 | solution.py:180
  237.5 2.9 convolution_bitcast_fusion.2
  248.0 2.9 convolution_bitcast_fusion.2
  258.6 2.9 convolution_bitcast_fusion.2
  262.9 1.5 fusion.65
  269.1 2.9 convolution_bitcast_fusion.2
  279.7 2.9 convolution_bitcast_fusion.2
  284.0 1.5 fusion.65
  290.3 2.9 convolution_bitcast_fusion.2
  300.8 2.9 convolution_bitcast_fusion.2
  305.1 1.5 fusion.65
  311.4 2.9 convolution_bitcast_fusion.2
  321.9 2.9 convolution_bitcast_fusion.2
  326.3 1.5 fusion.65
  332.5 2.9 convolution_bitcast_fusion.2
  343.1 2.9 convolution_bitcast_fusion.2
  347.4 1.5 fusion.65
  353.6 2.9 convolution_bitcast_fusion.2
  364.2 2.9 convolution_bitcast_fusion.2
  368.5 1.5 fusion.65
  374.7 2.9 convolution_bitcast_fusion.2
  385.3 2.9 convolution_bitcast_fusion.2
  395.9 2.9 convolution_bitcast_fusion.2
  411.9 75.3 %all_to_all.41 = f32[8,3,4,16,512]{4,2,1,3,0:T(4,128)S(1)} all-to-all(f32[8,3,4,16,512]{4,2,1,3,0:T(4,128)S(1)} %fusion.30), channel_id=1, replica_groups=mesh['freq'=8,'lat'=8,'lon'=4] {'freq'}, dimensions={0} | all-to-all | bytes 6291456 | tf_op jit(solution)/shard_map/all_to_all | solution.py:192
  487.3 2.6 copy.117
  (370 shorter events, 100.9 us)
Async XLA Ops:
  2.3 3.4 copy-start.5
  3.9 2.2 copy-start.1
  5.7 2.7 copy-start.2
  6.0 2.4 copy-start
  8.5 6.7 %collective-permute-start = (f32[5,4,1,512]{3,0,2,1:T(8,128)S(1)}, f32[5,4,1,512]{3,0,2,1:T(8,128)S(1)}, u32[]{:S(2)}, u32[]{:S(2)}) collective-permute-start(f32[5,4,1,512]{3,0,2,1:T(8,128)S(1)} %copy.102), channel_id=1, source_target_pairs={{0,4},{4,8},{8,12},{12,16},{16,20},{20,24},{24,28},{28,0},{1,5},{5... | collective-permute-start | bytes 122888 | tf_op jit(solution)/shard_map/ppermute | solution.py:21
  11.8 5.8 %collective-permute-start.1 = (f32[5,4,1,512]{3,0,2,1:T(8,128)S(1)}, f32[5,4,1,512]{3,0,2,1:T(8,128)S(1)}, u32[]{:S(2)}, u32[]{:S(2)}) collective-permute-start(f32[5,4,1,512]{3,0,2,1:T(8,128)S(1)} %copy.103), channel_id=1, source_target_pairs={{4,0},{8,4},{12,8},{16,12},{20,16},{24,20},{28,24},{0,28},{5,1},{9... | collective-permute-start | bytes 122888 | tf_op jit(solution)/shard_map/ppermute | solution.py:24
  21.2 3.4 collective-permute-start.2
  22.4 3.6 collective-permute-start.3
  42.1 83.4 %all-to-all-start = ((f32[3,4,128,512]{3,1,0,2:T(4,128)}), f32[3,4,128,512]{3,1,0,2:T(4,128)S(1)}, u32[]{:S(2)}, u32[]{:S(2)}) async-start(f32[3,4,128,512]{3,1,0,2:T(4,128)} %copy.110), calls=%async_computation | async-start | bytes 6291456 | tf_op jit(solution)/shard_map/all_to_all | solution.py:164
  50.6 4.0 copy-start.4
  125.5 101.3 %all-to-all-start.1 = ((f32[4,4,128,512]{3,1,0,2:T(4,128)}), f32[4,4,128,512]{3,1,0,2:T(4,128)}, u32[]{:S(2)}, u32[]{:S(2)}) async-start(f32[4,4,128,512]{3,1,0,2:T(4,128)} %pad_maximum_fusion.1), calls=%async_computation.1 | async-start | bytes 8388608 | tf_op jit(solution)/shard_map/all_to_all | solution.py:163
  406.4 5.1 %copy-start.3 = (f32[16,3,32,512]{3,2,1,0:T(8,128)S(1)}, f32[16,3,32,512]{3,2,1,0:T(8,128)}, u32[]{:S(2)}) copy-start(f32[16,3,32,512]{3,2,1,0:T(8,128)} %get-tuple-element.135) | copy-start | bytes 9437188
